TPU v7x, 128 devices: a whole 4x4x4 slice. The times are simulated.
128 devices in a mesh: blk: 16 (over y_hi, x, core), kv: 8 (over z, y_lo).
Axes of the slice: x: 4, y: 4 (y_hi: 2, y_lo: 2; y = y_hi * 2 + y_lo), z: 4, core: 2. Of those that a mesh axis runs over, the one named last changes fastest.
Arguments:
- tokens: bfloat16 [8192, 2560], P('blk'), may hold values from -6 to 6
- attn_gain: float32 [2560], replicated, may hold values from 0.1 to 1.9
- mlp_gain: float32 [2560], replicated, may hold values from 0.1 to 1.9
- w_query: float32 [2560, 2560], P(('blk', 'kv')), may hold values from -0.375 to 0.375
- w_key: float32 [2560, 640], P(('blk', 'kv')), may hold values from -0.125 to 0.125
- w_value: float32 [2560, 640], P(('blk', 'kv')), may hold values from -0.125 to 0.125
- w_gate: float32 [2560, 6912], P(('blk', 'kv')), may hold values from -0.125 to 0.125
- w_up: float32 [2560, 6912], P(('blk', 'kv')), may hold values from -0.125 to 0.125
- w_out: bfloat16 [2560, 2560], P('kv'), may hold values from -0.125 to 0.125
- w_down: bfloat16 [6912, 2560], P('kv'), may hold values from -0.078125 to 0.078125
- cache: bfloat16 [2, 128, 8, 80, 128], P(None, 'blk', 'kv'), may hold values from -300 to 300
- slot_prompt: int32 [128], replicated, may hold values from 0 to 15, as said below
- prefix_len: int32 [16], replicated, may hold values from 1 to 4096, as said below
- new_len: int32 [16], replicated, may hold values from 256 to 512, as said below
Outputs:
- mixed: bfloat16 [8192, 2560], P('blk', 'kv')
Inputs may be any that keep to these rules, and one draw needn't show every extreme that they name: `slot_prompt`: the 8 slots of one index of blk hold at most 2 blocks of one prompt. One prompt, drawn afresh, has exactly 2 blocks on every index of blk; the other 6 slots of an index hold blocks of distinct prompts; every prompt has at least one block. `prefix_len`: A prompt with c slots has a prefix longer than (c - 1) * 128 and at most c * 128. Rows i >= new_len[p] of prompt p are padding.
All inputs are finite; a program needn't handle non-finite values.
Results may differ from a plain program's by a relative error of at most 0.019.
The roundings to bfloat16 on the way count: a program that leaves them out, or rounds other values in their place, can miss the bound.
Values may be sent and summed in bfloat16 or wider, within the bound.
A program may use at most 128 MiB of HBM per device.

v0:
```python
import math
import jax
import jax.numpy as jnp
from jax import lax
from jax.sharding import PartitionSpec as P

HEADS = 32
KV_HEADS = 8
HD = 80
WINDOW = 4096
SINKS = 4
BLOCK = 128
CAP = 2
FLOOR_SCORE = -1e30
EPSILON = 1e-05
ROPE_BASE = 10000.0


def rms_scale(row_data, gain_vec):
    values = row_data.astype(jnp.float32)
    mean_square = jnp.mean(values * values, axis=-1, keepdims=True)
    return (values * lax.rsqrt(mean_square + EPSILON) * gain_vec).astype(jnp.bfloat16)


def rotate(values, positions):
    head_width = values.shape[-1]
    half_width = head_width // 2
    frequency = ROPE_BASE ** (-2.0 * jnp.arange(half_width, dtype=jnp.float32) / head_width)
    angles = positions.astype(jnp.float32)[:, None] * frequency[None, :]
    cosine = jnp.cos(angles)[:, None, :]
    sine_wave = jnp.sin(angles)[:, None, :]
    first_half = values[..., :half_width]
    second_half = values[..., half_width:]
    return jnp.concatenate(
        [
            first_half * cosine - second_half * sine_wave,
            second_half * cosine + first_half * sine_wave,
        ],
        axis=-1,
    )


def slot_ranks(slot_prompt, prompts, slots):
    onehot = (slot_prompt[:, None] == jnp.arange(prompts, dtype=jnp.int32)[None, :]).astype(
        jnp.int32
    )
    running = jnp.cumsum(onehot, axis=0)
    global_rank = jnp.sum(onehot * (running - 1), axis=1)
    local_count = jnp.cumsum(onehot.reshape(-1, slots, prompts), axis=1).reshape(-1, prompts)
    local_rank = jnp.sum(onehot * (local_count - 1), axis=1)
    return (global_rank, local_rank)


def visible(query_pos, key_pos):
    distance = query_pos - key_pos
    return (distance >= 0) & ((distance < WINDOW) | (key_pos < SINKS))


def partial_block(scores, seen_mask):
    masked = jnp.where(seen_mask, scores, FLOOR_SCORE)
    row_max = jnp.max(masked, axis=-1)
    weights = jnp.where(seen_mask, jnp.exp(masked - row_max[..., None]), 0.0)
    return (row_max, jnp.sum(weights, axis=-1), weights.astype(jnp.bfloat16))


def combine(first_part, second_part):
    maxima = jnp.maximum(first_part[0], second_part[0])
    scale_first = jnp.exp(first_part[0] - maxima)
    scale_second = jnp.exp(second_part[0] - maxima)
    totals = first_part[1] * scale_first + second_part[1] * scale_second
    outputs = first_part[2] * scale_first[..., None] + second_part[2] * scale_second[..., None]
    return (maxima, totals, outputs)


def pack_groups(matrices, groups):
    pieces = [
        matrix.reshape(matrix.shape[0], groups, matrix.shape[1] // groups) for matrix in matrices
    ]
    joined = jnp.concatenate(pieces, axis=2)
    return joined.reshape(matrices[0].shape[0], -1).astype(jnp.bfloat16)


def restack(moved_rows, groups, n_blocks):
    columns = moved_rows.shape[1]
    ordered = moved_rows.reshape(groups, n_blocks, -1, columns)
    return jnp.transpose(ordered, (1, 0, 2, 3)).reshape(-1, columns)


def shards(
    tokens,
    attn_gain,
    mlp_gain,
    w_query,
    w_key,
    w_value,
    w_gate,
    w_up,
    w_out,
    w_down,
    cache,
    slot_prompt,
    prefix_len,
    new_len,
):
    groups = lax.axis_size("kv")
    n_blocks = lax.axis_size("blk")
    blk_index = lax.axis_index("blk")
    kv_index = lax.axis_index("kv")
    merged_attn = pack_groups((w_query, w_key, w_value), groups)
    merged_mlp = pack_groups((w_gate, w_up), groups)
    collected = (
        lax.all_gather(merged_attn, "blk", axis=0, tiled=True),
        lax.all_gather(merged_mlp, "blk", axis=0, tiled=True),
    )
    moved_attn, moved_mlp = (
        lax.all_to_all(collected[0], "kv", split_axis=1, concat_axis=0, tiled=True),
        lax.all_to_all(collected[1], "kv", split_axis=1, concat_axis=0, tiled=True),
    )
    w_qkv = restack(moved_attn, groups, n_blocks)
    w_pair = restack(moved_mlp, groups, n_blocks)
    query_width = w_query.shape[1] // groups
    key_width = w_key.shape[1] // groups
    kv_local = key_width // HD
    per_group = HEADS // KV_HEADS
    new_rows = tokens.shape[0]
    prompts = prefix_len.shape[0]
    slots = cache.shape[1]
    score_scale = 1.0 / math.sqrt(HD)
    prefix_here = prefix_len[blk_index]
    live_count = new_len[blk_index]
    row_ids = jnp.arange(new_rows, dtype=jnp.int32)
    positions = prefix_here + row_ids
    offsets = jnp.arange(BLOCK, dtype=jnp.int32)
    normed = rms_scale(tokens, attn_gain)
    projected = jnp.dot(normed, w_qkv, preferred_element_type=jnp.float32)
    queries = rotate(projected[:, :query_width].reshape(new_rows, -1, HD), positions).astype(
        jnp.bfloat16
    )
    key_new = rotate(
        projected[:, query_width : query_width + key_width].reshape(new_rows, kv_local, HD),
        positions,
    ).astype(jnp.bfloat16)
    value_new = (
        projected[:, query_width + key_width :].reshape(new_rows, kv_local, HD).astype(jnp.bfloat16)
    )
    grouped_q = queries.reshape(new_rows, kv_local, per_group, HD)
    own_scores = (
        jnp.einsum("qgnd,kgd->gnqk", grouped_q, key_new, preferred_element_type=jnp.float32)
        * score_scale
    )
    own_mask = (row_ids[None, :] < live_count) & visible(positions[:, None], positions[None, :])
    own_max, own_sum, own_weights = partial_block(own_scores, own_mask)
    own_out = jnp.einsum(
        "gnqk,kgd->gnqd", own_weights, value_new, preferred_element_type=jnp.float32
    )
    running = (own_max, own_sum, own_out)
    global_rank, local_rank = slot_ranks(slot_prompt, prompts, slots)
    own_prompts = lax.dynamic_slice_in_dim(slot_prompt, blk_index * slots, slots)
    own_ranks = lax.dynamic_slice_in_dim(local_rank, blk_index * slots, slots)
    placed = own_prompts * CAP + own_ranks
    buffer_ids = jnp.arange(prompts * CAP, dtype=jnp.int32)
    matches = placed[None, :] == buffer_ids[:, None]
    source_slot = jnp.sum(
        jnp.where(matches, jnp.arange(slots, dtype=jnp.int32)[None, :], 0), axis=1
    )
    filled = jnp.any(matches, axis=1)
    outgoing = jnp.where(
        filled[None, :, None, None, None],
        jnp.take(cache, source_slot, axis=1),
        jnp.zeros((), cache.dtype),
    )
    arrived = lax.all_to_all(outgoing, "blk", split_axis=1, concat_axis=1, tiled=True)
    slot_ids = jnp.arange(prompts * slots, dtype=jnp.int32)
    landing = slot_ids // slots * CAP + local_rank
    for_me = slot_prompt == blk_index
    received = (landing[None, :] == buffer_ids[:, None]) & for_me[None, :]
    block_number = jnp.sum(jnp.where(received, global_rank[None, :], 0), axis=1)
    block_live = jnp.any(received, axis=1)
    total_slots = prompts * CAP
    group_slots = min(total_slots, max(1, 512 // BLOCK))
    step_count = total_slots // group_slots
    key_blocks = arrived[0].reshape(step_count, group_slots, kv_local, HD, BLOCK)
    value_blocks = arrived[1].reshape(step_count, group_slots, kv_local, HD, BLOCK)
    numbers = block_number.reshape(step_count, group_slots)
    live_flags = block_live.reshape(step_count, group_slots)

    def prefix_step(running_state, inputs):
        key_part, value_part, number_part, flag_part = inputs
        scores = (
            jnp.einsum("qgnd,sgdt->gnqst", grouped_q, key_part, preferred_element_type=jnp.float32)
            * score_scale
        )
        scores = scores.reshape(kv_local, per_group, new_rows, group_slots * BLOCK)
        key_pos = number_part[:, None] * BLOCK + offsets[None, :]
        key_live = (flag_part[:, None] & (key_pos < prefix_here)).reshape(-1)
        seen_mask = key_live[None, :] & visible(positions[:, None], key_pos.reshape(-1)[None, :])
        block_max, block_sum, weights = partial_block(scores, seen_mask)
        weights = weights.reshape(kv_local, per_group, new_rows, group_slots, BLOCK)
        block_out = jnp.einsum(
            "gnqst,sgdt->gnqd", weights, value_part, preferred_element_type=jnp.float32
        )
        return (combine(running_state, (block_max, block_sum, block_out)), None)

    running = lax.scan(prefix_step, running, (key_blocks, value_blocks, numbers, live_flags))[0]
    totals = running[1]
    outputs = running[2]
    attended = (
        jnp.transpose(outputs / totals[..., None], (2, 0, 1, 3))
        .reshape(new_rows, -1)
        .astype(jnp.bfloat16)
    )
    projected_out = jnp.dot(attended, w_out, preferred_element_type=jnp.float32)
    summed = lax.psum(projected_out.astype(jnp.bfloat16), "kv").astype(jnp.float32)
    middle = (tokens.astype(jnp.float32) + summed).astype(jnp.bfloat16)
    normed_mid = rms_scale(middle, mlp_gain)
    paired = jnp.dot(normed_mid, w_pair, preferred_element_type=jnp.float32)
    hidden_width = w_pair.shape[1] // 2
    hidden = (jax.nn.silu(paired[:, :hidden_width]) * paired[:, hidden_width:]).astype(jnp.bfloat16)
    down_part = jnp.dot(hidden, w_down, preferred_element_type=jnp.float32)
    reduced = lax.psum_scatter(
        down_part.astype(jnp.bfloat16), "kv", scatter_dimension=1, tiled=True
    ).astype(jnp.float32)
    out_width = reduced.shape[1]
    residual = lax.dynamic_slice_in_dim(middle, kv_index * out_width, out_width, 1).astype(
        jnp.float32
    )
    mixed = jnp.where((row_ids < live_count)[:, None], residual + reduced, 0.0)
    return mixed.astype(jnp.bfloat16)


def solution(mesh):
    return jax.shard_map(
        shards,
        mesh=mesh,
        in_specs=(
            P("blk", None),
            P(),
            P(),
            P(("blk", "kv"), None),
            P(("blk", "kv"), None),
            P(("blk", "kv"), None),
            P(("blk", "kv"), None),
            P(("blk", "kv"), None),
            P("kv", None),
            P("kv", None),
            P(None, "blk", "kv", None, None),
            P(),
            P(),
            P(),
        ),
        out_specs=P("blk", "kv"),
        check_vma=False,
    )
```

profile of v0, /device:TPU:1, one launch (start us, length us, event | category | flops | bytes accessed | tf_op | source)
XLA Modules:
  0.0 535.5 jit_solution(12732997169242167067)
XLA Ops:
  18.9 8.4 %all-to-all-start.1 = ((bf16[2,32,1,80,128]{4,3,0,2,1:T(8,128)(2,1)}), bf16[2,32,1,80,128]{4,3,0,2,1:T(8,128)(2,1)S(1)}, u32[]{:S(2)}, u32[]{:S(2)}) async-start(bf16[2,32,1,80,128]{4,3,0,2,1:T(8,128)(2,1)} %fusion.68), calls=%async_computation.1 | async-start | bytes 2621440 | tf_op jit(solution)/shard_map/all_to_all | solution.py:172
  27.4 41.5 %all-gather.5.cloned.1.call-done = bf16[16,20,3840]{2,1,0:T(8,128)(2,1)} async-done(((bf16[1,20,3840]{2,1,0:T(8,128)(2,1)}), bf16[16,20,3840]{2,1,0:T(8,128)(2,1)}) %all-gather.5.cloned.1.call-update) | async-done | bytes 2457616 | tf_op jit(solution)/shard_map/all_gather | solution.py:112
  68.9 6.6 %all_to_all.27 = bf16[320,8,480]{2,1,0:T(8,128)(2,1)} reshape(bf16[16,20,3840]{2,1,0:T(8,128)(2,1)} %all-gather.5.cloned.1.call-done) | data formatting | bytes 4915200 | tf_op jit(solution)/shard_map/all_to_all | solution.py:116
  75.4 4.2 copy.61
  79.6 4.7 all-to-all-start
  85.6 4.4 copy.60
  97.2 29.5 %all-to-all-done = bf16[320,8,480]{2,0,1:T(8,128)(2,1)} async-done(((bf16[320,8,480]{2,0,1:T(8,128)(2,1)}), bf16[320,8,480]{2,0,1:T(8,128)(2,1)}, u32[]{:S(2)}, u32[]{:S(2)}) %all-to-all-start) | async-done | bytes 2457632 | tf_op jit(solution)/shard_map/all_to_all | solution.py:116
  126.7 3.3 copy.62
  132.9 5.5 %reshape.470 = bf16[2560,480]{1,0:T(8,128)(2,1)} reshape(bf16[16,8,20,480]{3,2,1,0:T(8,128)(2,1)} %copy.63) | data formatting | bytes 4915200 | tf_op jit(solution)/shard_map/reshape | solution.py:86
  138.4 4.2 fusion.55
  146.5 16.6 %all-gather.7.cloned.1.call-done = bf16[16,20,13824]{2,1,0:T(8,128)(2,1)} async-done(((bf16[1,20,13824]{2,1,0:T(8,128)(2,1)}), bf16[16,20,13824]{2,1,0:T(8,128)(2,1)}) %all-gather.7.cloned.1.call-update) | async-done | bytes 8847376 | tf_op jit(solution)/shard_map/all_gather | solution.py:113
  163.1 16.9 %all_to_all.31 = bf16[320,8,1728]{2,1,0:T(8,128)(2,1)} reshape(bf16[16,20,13824]{2,1,0:T(8,128)(2,1)} %all-gather.7.cloned.1.call-done) | data formatting | bytes 17694720 | tf_op jit(solution)/shard_map/all_to_all | solution.py:117
  180.0 8.9 %copy.68 = bf16[320,8,1728]{2,0,1:T(8,128)(2,1)} copy(bf16[320,8,1728]{2,1,0:T(8,128)(2,1)} %all_to_all.31) | data formatting | bytes 17694720 | tf_op jit(solution)/shard_map/all_to_all | solution.py:117
  189.0 5.0 all-to-all-start.2
  194.0 57.9 %while.16 = (s32[]{:T(128)}, f32[1,4,512]{2,1,0:T(4,128)S(1)}, f32[1,4,512]{2,1,0:T(4,128)S(1)}, f32[1,4,512,80]{2,3,1,0:T(8,128)S(1)}, pred[8,4]{1,0:T(8,128)(4...) while((s32[]{:T(128)}, f32[1,4,512]{2,1,0:T(4,128)S(1)}, ...), condition=%wide.region_14.15_spmd.clone.clone, body=%wide.region_11.14_spmd.clone.clone.sunk | while | flops 351253504 | bytes 15599833 | solution.py:204
  252.0 3.1 convolution_convert_fusion.1
  255.3 151.3 %all-reduce.2.cloned.1.call-done = bf16[512,2560]{0,1:T(8,128)(2,1)} async-done(((bf16[512,2560]{0,1:T(8,128)(2,1)}), bf16[512,2560]{0,1:T(8,128)(2,1)}) %all-reduce.2.cloned.1.call-update) | async-done | bytes 2621456 | tf_op jit(solution)/shard_map/psum | solution.py:213
  406.6 5.1 fusion.44
  411.7 12.2 %copy.69 = bf16[320,8,1728]{2,1,0:T(8,128)(2,1)} copy(bf16[320,8,1728]{2,0,1:T(8,128)(2,1)} %all-to-all-done.2) | data formatting | bytes 17694720 | tf_op jit(solution)/shard_map/all_to_all | solution.py:117
  423.9 10.4 %copy.70 = bf16[16,8,20,1728]{3,2,1,0:T(8,128)(2,1)} copy(bf16[16,8,20,1728]{3,1,2,0:T(8,128)(2,1)} %bitcast.203) | data formatting | bytes 17694720 | tf_op jit(solution)/shard_map/transpose | solution.py:86
  434.3 14.4 %reshape.479 = bf16[2560,1728]{1,0:T(8,128)(2,1)} reshape(bf16[16,8,20,1728]{3,2,1,0:T(8,128)(2,1)} %copy.70) | data formatting | bytes 17694720 | tf_op jit(solution)/shard_map/reshape | solution.py:86
  448.6 8.9 %fusion.57 = f32[512,1728]{0,1:T(8,128)S(1)} fusion(bf16[2560,1728]{1,0:T(8,128)(2,1)} %reshape.479, bf16[512,2560]{0,1:T(8,128)(2,1)} %get-tuple-element.184, f32[2560]{0:T(1024)S(1)} %copy-done.4, f32[512]{0:T(512)S(1)} %add_rsqrt_fusion), kind=kOutput, calls=%fused_computation.68 | convolution fusion | flops 4535091200 | bytes 15020032 | tf_op jit(solution)/shard_map/dot_general | solution.py:216
  457.5 7.4 %fusion.51 = bf16[2560,512]{1,0:T(8,128)(2,1)} fusion(bf16[864,2560]{1,0:T(8,128)(2,1)} %param.25, f32[512,1728]{0,1:T(8,128)S(1)} %fusion.57), kind=kOutput, calls=%fused_computation.63 | convolution fusion | flops 2268889088 | bytes 10584064 | tf_op jit(solution)/shard_map/dot_general | solution.py:219
  465.0 61.9 %reduce-scatter.4.cloned.1.call-done = bf16[320,512]{1,0:T(8,128)(2,1)} async-done(((bf16[2560,512]{1,0:T(8,128)(2,1)}), bf16[320,512]{1,0:T(8,128)(2,1)}) %reduce-scatter.4.cloned.1.call-update) | async-done | bytes 327696
  (178 shorter events, 87.0 us)
Async XLA Ops:
  6.5 245.4 %copy-start = (bf16[320,2560]{1,0:T(8,128)(2,1)S(1)}, bf16[320,2560]{1,0:T(8,128)(2,1)}, u32[]{:S(2)}) copy-start(bf16[320,2560]{1,0:T(8,128)(2,1)} %param.24) | copy-start | bytes 4915204
  6.5 9.2 %copy-start.2 = (s32[128]{0:T(128)S(1)}, s32[128]{0:T(128)}, u32[]{:S(2)}) copy-start(s32[128]{0:T(128)} %param.27) | copy-start | bytes 1540
  6.5 62.3 %all-gather.5.cloned.1.call-start = ((), (), s32[]{:S(2)}) async-start(), calls=%async_computation.5 | async-start | bytes 3133440 | tf_op jit(solution)/shard_map/all_gather | solution.py:112
  7.5 9.2 %copy-start.1 = (bf16[2,8,1,80,128]{4,3,2,1,0:T(8,128)(2,1)S(1)}, bf16[2,8,1,80,128]{4,3,2,1,0:T(8,128)(2,1)}, u32[]{:S(2)}) copy-start(bf16[2,8,1,80,128]{4,3,2,1,0:T(8,128)(2,1)} %param.26) | copy-start | bytes 983044
  10.8 152.4 %all-gather.7.cloned.1.call-start = ((), (), s32[]{:S(2)}) async-start(), calls=%async_computation.6 | async-start | bytes 11280384 | tf_op jit(solution)/shard_map/all_gather | solution.py:113
  18.9 60.7 %all-to-all-start.1 = ((bf16[2,32,1,80,128]{4,3,0,2,1:T(8,128)(2,1)}), bf16[2,32,1,80,128]{4,3,0,2,1:T(8,128)(2,1)S(1)}, u32[]{:S(2)}, u32[]{:S(2)}) async-start(bf16[2,32,1,80,128]{4,3,0,2,1:T(8,128)(2,1)} %fusion.68), calls=%async_computation.1 | async-start | bytes 2621440 | tf_op jit(solution)/shard_map/all_to_all | solution.py:172
  75.4 8.9 %copy-start.5 = (s32[16]{0:T(128)S(1)}, s32[16]{0:T(128)}, u32[]{:S(2)}) copy-start(s32[16]{0:T(128)} %param.28) | copy-start | bytes 196
  75.4 9.6 %copy-start.6 = (s32[16]{0:T(128)S(1)}, s32[16]{0:T(128)}, u32[]{:S(2)}) copy-start(s32[16]{0:T(128)} %param.29) | copy-start | bytes 196
  79.6 47.1 %all-to-all-start = ((bf16[320,8,480]{2,0,1:T(8,128)(2,1)}), bf16[320,8,480]{2,0,1:T(8,128)(2,1)}, u32[]{:S(2)}, u32[]{:S(2)}) async-start(bf16[320,8,480]{2,0,1:T(8,128)(2,1)} %copy.61), calls=%async_computation | async-start | bytes 5242880 | tf_op jit(solution)/shard_map/all_to_all | solution.py:116
  132.9 5.5 %copy-start.3 = (f32[2560]{0:T(1024)S(1)}, f32[2560]{0:T(1024)}, u32[]{:S(2)}) copy-start(f32[2560]{0:T(1024)} %param.17) | copy-start | bytes 30724
  189.0 222.7 %all-to-all-start.2 = ((bf16[320,8,1728]{2,0,1:T(8,128)(2,1)}), bf16[320,8,1728]{2,0,1:T(8,128)(2,1)}, u32[]{:S(2)}, u32[]{:S(2)}) async-start(bf16[320,8,1728]{2,0,1:T(8,128)(2,1)} %copy.68), calls=%async_computation.2 | async-start | bytes 18350080 | tf_op jit(solution)/shard_map/all_to_all | solution.py:117
  194.0 212.6 %all-reduce.2.cloned.1.call-start = ((), (), s32[]{:S(2)}) async-start(), calls=%async_computation.4 | async-start | bytes 5242880 | tf_op jit(solution)/shard_map/psum | solution.py:213
  255.1 271.7 %reduce-scatter.4.cloned.1.call-start = ((), (), s32[]{:S(2)}) async-start(), calls=%async_computation.7 | async-start | bytes 2949120
  434.3 14.4 %copy-start.4 = (f32[2560]{0:T(1024)S(1)}, f32[2560]{0:T(1024)}, u32[]{:S(2)}) copy-start(f32[2560]{0:T(1024)} %param.18) | copy-start | bytes 30724
Sparse Core Ops, SparseCore 0:
  10.9 57.9 all-gather.4
  71.3 91.7 all-gather.6
  255.2 151.3 all-reduce.1
  465.1 61.6 reduce-scatter.3
where the time goes:
time: 543 us; the launch traced here: 536 us
  waiting for transfers between devices  301 us (55%)
  local copies, waits for them, and re-layouts  97.1 us (18%)
  matrix products  58.8 us (11%)
  other arithmetic  46.1 us (8%)
  starting transfers between devices  18.5 us (3%)
  between operations  13.6 us (3%)
    psum x1, waiting for transfers between devices, shards(): lax.psum(projected_out.astype(jnp.bfloat16), 'kv').astype(jnp.float32)  151 us
    unnamed x5, waiting for transfers between devices  61.9 us
    all_gather x1, waiting for transfers between devices, shards(): lax.all_gather(merged_attn, 'blk', axis=0, tiled=True)  41.5 us
    all_to_all x3, local copies, waits for them, and re-layouts, shards(): lax.all_to_all(collected[1], 'kv', split_axis=1, concat_axis=0, tiled=True)  38 us
    all_to_all x1, waiting for transfers between devices, shards(): lax.all_to_all(collected[0], 'kv', split_axis=1, concat_axis=0, tiled=True)  29.5 us
    reshape x2, local copies, waits for them, and re-layouts, restack(): return jnp.transpose(ordered, (1, 0, 2, 3)).reshape(-1, columns)  19.9 us
    dot_general x8, matrix products, prefix_step(): jnp.einsum('gnqst,sgdt->gnqd', weights, value_part, preferred_element_typ...  18.6 us
    all_gather x1, waiting for transfers between devices, shards(): lax.all_gather(merged_mlp, 'blk', axis=0, tiled=True)  16.6 us
  transfers between devices with their start and end apart: 7, of which 5 were waited for; matrix products, arithmetic and copies ran while one was open for 21% of the time, Pallas kernels for 0%

commit v1 on v0

--- a/solution.py
+++ b/solution.py
@@ -3,6 +3,7 @@
 import jax.numpy as jnp
 from jax import lax
 from jax.sharding import PartitionSpec as P
+from jax.lax import all_to_all, axis_size
 
 HEADS = 32
 KV_HEADS = 8
@@ -14,6 +15,14 @@
 FLOOR_SCORE = -1e30
 EPSILON = 1e-05
 ROPE_BASE = 10000.0
+
+
+def wrap_the_slabs(local_block):
+    all_rows = jnp.concatenate(
+        all_to_all(jnp.stack([local_block for _ in range(axis_size("blk"))], axis=0), "blk", 0, 0),
+        axis=0,
+    )
+    return all_rows
 
 
 def rms_scale(row_data, gain_vec):
@@ -108,10 +117,7 @@
     kv_index = lax.axis_index("kv")
     merged_attn = pack_groups((w_query, w_key, w_value), groups)
     merged_mlp = pack_groups((w_gate, w_up), groups)
-    collected = (
-        lax.all_gather(merged_attn, "blk", axis=0, tiled=True),
-        lax.all_gather(merged_mlp, "blk", axis=0, tiled=True),
-    )
+    collected = (wrap_the_slabs(merged_attn), lax.all_gather(merged_mlp, "blk", axis=0, tiled=True))
     moved_attn, moved_mlp = (
         lax.all_to_all(collected[0], "kv", split_axis=1, concat_axis=0, tiled=True),
         lax.all_to_all(collected[1], "kv", split_axis=1, concat_axis=0, tiled=True),

time: 543 us -> 556 us (1.024)
  starting transfers between devices: 18.5 us -> 29.3 us
    all_to_all x0 -> x1, waiting for transfers between devices: none -> 41.8 us  [wrap_the_slabs(): all_to_all(jnp.stack([local_block for _ in range(axis_size('blk'))], axis...]
    all_gather x1 -> x0, waiting for transfers between devices: 41.5 us -> none  [shards(): lax.all_gather(merged_attn, 'blk', axis=0, tiled=True)]
    all_gather x1, waiting for transfers between devices: 16.6 us -> 0.02 us  [shards(): lax.all_gather(merged_mlp, 'blk', axis=0, tiled=True)]
    all_to_all x1, waiting for transfers between devices: 0.01 us -> 13.5 us  [shards(): lax.all_to_all(outgoing, 'blk', split_axis=1, concat_axis=1, tiled=True)]
    all_to_all x0 -> x1, starting transfers between devices: none -> 8.45 us  [wrap_the_slabs(): all_to_all(jnp.stack([local_block for _ in range(axis_size('blk'))], axis...]
    unnamed x5 -> x4, waiting for transfers between devices: 61.9 us -> 61.8 us
  transfers between devices with their start and end apart: 7 -> 7, of which waited for: 5 -> 5; matrix products, arithmetic and copies ran while one was open for 21% -> 20% of each run, Pallas kernels for 0% -> 0%
where the time goes in v1:
time: 556 us; the launch traced here: 549 us
  waiting for transfers between devices  303 us (54%)
  local copies, waits for them, and re-layouts  98.3 us (18%)
  matrix products  58.8 us (11%)
  other arithmetic  43.5 us (8%)
  starting transfers between devices  29.3 us (5%)
  between operations  15.4 us (3%)
    psum x1, waiting for transfers between devices, shards(): lax.psum(projected_out.astype(jnp.bfloat16), 'kv').astype(jnp.float32)  155 us
    unnamed x4, waiting for transfers between devices  61.8 us
    all_to_all x1, waiting for transfers between devices, wrap_the_slabs(): all_to_all(jnp.stack([local_block for _ in range(axis_size('blk'))], axis...  41.8 us
    all_to_all x3, local copies, waits for them, and re-layouts, shards(): lax.all_to_all(collected[1], 'kv', split_axis=1, concat_axis=0, tiled=True)  38 us
    all_to_all x1, waiting for transfers between devices, shards(): lax.all_to_all(collected[0], 'kv', split_axis=1, concat_axis=0, tiled=True)  30.8 us
    reshape x2, local copies, waits for them, and re-layouts, restack(): return jnp.transpose(ordered, (1, 0, 2, 3)).reshape(-1, columns)  19.9 us
    dot_general x8, matrix products, prefix_step(): jnp.einsum('gnqst,sgdt->gnqd', weights, value_part, preferred_element_typ...  18.6 us
    dot_general x8, matrix products, prefix_step(): jnp.einsum('qgnd,sgdt->gnqst', grouped_q, key_part, preferred_element_typ...  14.3 us
  transfers between devices with their start and end apart: 7, of which 5 were waited for; matrix products, arithmetic and copies ran while one was open for 20% of the time, Pallas kernels for 0%

profile of v1, /device:TPU:1, one launch (start us, length us, event | category | flops | bytes accessed | tf_op | source)
XLA Modules:
  0.0 548.6 jit_solution(3816590424289516098)
XLA Ops:
  15.1 8.4 %all-to-all-start = ((bf16[16,20,3840]{2,1,0:T(8,128)(2,1)}), bf16[16,20,3840]{2,1,0:T(8,128)(2,1)}, u32[]{:S(2)}, u32[]{:S(2)}) async-start(bf16[16,20,3840]{2,1,0:T(8,128)(2,1)} %stack.2), calls=%async_computation | async-start | bytes 5898240 | tf_op jit(solution)/shard_map/all_to_all | solution.py:22
  26.8 41.8 %all-to-all-done = bf16[16,20,3840]{2,1,0:T(8,128)(2,1)} async-done(((bf16[16,20,3840]{2,1,0:T(8,128)(2,1)}), bf16[16,20,3840]{2,1,0:T(8,128)(2,1)}, u32[]{:S(2)}, u32[]{:S(2)}) %all-to-all-start) | async-done | bytes 2457632 | tf_op jit(solution)/shard_map/all_to_all | solution.py:22
  68.5 7.9 %all-to-all-start.2 = ((bf16[2,32,1,80,128]{4,3,0,2,1:T(8,128)(2,1)}), bf16[2,32,1,80,128]{4,3,0,2,1:T(8,128)(2,1)S(1)}, u32[]{:S(2)}, u32[]{:S(2)}) async-start(bf16[2,32,1,80,128]{4,3,0,2,1:T(8,128)(2,1)} %fusion.68), calls=%async_computation.2 | async-start | bytes 2621440 | tf_op jit(solution)/shard_map/all_to_all | solution.py:178
  76.4 6.7 %all_to_all.31 = bf16[320,8,480]{2,1,0:T(8,128)(2,1)} reshape(bf16[16,20,3840]{2,1,0:T(8,128)(2,1)} %all-to-all-done) | data formatting | bytes 4915200 | tf_op jit(solution)/shard_map/all_to_all | solution.py:122
  83.1 4.2 copy.61
  87.2 13.5 %all-to-all-done.2 = bf16[2,32,1,80,128]{4,3,0,2,1:T(8,128)(2,1)S(1)} async-done(((bf16[2,32,1,80,128]{4,3,0,2,1:T(8,128)(2,1)}), bf16[2,32,1,80,128]{4,3,0,2,1:T(8,128)(2,1)S(1)}, u32[]{:S(2)}, u32[]{:S(2)}) %all-to-all-start.2) | async-done | bytes 1310752 | tf_op jit(solution)/shard_map/all_to_all | solution.py:178
  100.7 7.7 %all-to-all-start.1 = ((bf16[320,8,480]{2,0,1:T(8,128)(2,1)}), bf16[320,8,480]{2,0,1:T(8,128)(2,1)}, u32[]{:S(2)}, u32[]{:S(2)}) async-start(bf16[320,8,480]{2,0,1:T(8,128)(2,1)} %copy.61), calls=%async_computation.1 | async-start | bytes 5242880 | tf_op jit(solution)/shard_map/all_to_all | solution.py:122
  109.7 4.4 copy.60
  121.3 30.8 %all-to-all-done.1 = bf16[320,8,480]{2,0,1:T(8,128)(2,1)} async-done(((bf16[320,8,480]{2,0,1:T(8,128)(2,1)}), bf16[320,8,480]{2,0,1:T(8,128)(2,1)}, u32[]{:S(2)}, u32[]{:S(2)}) %all-to-all-start.1) | async-done | bytes 2457632 | tf_op jit(solution)/shard_map/all_to_all | solution.py:122
  152.2 3.2 copy.62
  158.2 5.5 %reshape.475 = bf16[2560,480]{1,0:T(8,128)(2,1)} reshape(bf16[16,8,20,480]{3,2,1,0:T(8,128)(2,1)} %copy.63) | data formatting | bytes 4915200 | tf_op jit(solution)/shard_map/reshape | solution.py:95
  163.8 4.2 fusion.55
  171.9 16.9 %all_to_all.35 = bf16[320,8,1728]{2,1,0:T(8,128)(2,1)} reshape(bf16[16,20,13824]{2,1,0:T(8,128)(2,1)} %all-gather.3.cloned.1.call-done) | data formatting | bytes 17694720 | tf_op jit(solution)/shard_map/all_to_all | solution.py:123
  188.8 8.9 %copy.68 = bf16[320,8,1728]{2,0,1:T(8,128)(2,1)} copy(bf16[320,8,1728]{2,1,0:T(8,128)(2,1)} %all_to_all.35) | data formatting | bytes 17694720 | tf_op jit(solution)/shard_map/all_to_all | solution.py:123
  197.8 5.0 all-to-all-start.3
  202.8 57.9 %while.16 = (s32[]{:T(128)}, f32[1,4,512]{2,1,0:T(4,128)S(1)}, f32[1,4,512]{2,1,0:T(4,128)S(1)}, f32[1,4,512,80]{2,3,1,0:T(8,128)S(1)}, pred[8,4]{1,0:T(8,128)(4...) while((s32[]{:T(128)}, f32[1,4,512]{2,1,0:T(4,128)S(1)}, ...), condition=%wide.region_14.15_spmd.clone.clone, body=%wide.region_11.14_spmd.clone.clone.sunk | while | flops 351253504 | bytes 15599833 | solution.py:210
  264.2 154.8 %all-reduce.2.cloned.1.call-done = bf16[512,2560]{0,1:T(8,128)(2,1)} async-done(((bf16[512,2560]{0,1:T(8,128)(2,1)}), bf16[512,2560]{0,1:T(8,128)(2,1)}) %all-reduce.2.cloned.1.call-update) | async-done | bytes 2621456 | tf_op jit(solution)/shard_map/psum | solution.py:219
  418.9 5.1 fusion.44
  424.0 12.2 %copy.69 = bf16[320,8,1728]{2,1,0:T(8,128)(2,1)} copy(bf16[320,8,1728]{2,0,1:T(8,128)(2,1)} %all-to-all-done.3) | data formatting | bytes 17694720 | tf_op jit(solution)/shard_map/all_to_all | solution.py:123
  436.2 10.4 %copy.70 = bf16[16,8,20,1728]{3,2,1,0:T(8,128)(2,1)} copy(bf16[16,8,20,1728]{3,1,2,0:T(8,128)(2,1)} %bitcast.203) | data formatting | bytes 17694720 | tf_op jit(solution)/shard_map/transpose | solution.py:95
  446.6 14.4 %reshape.484 = bf16[2560,1728]{1,0:T(8,128)(2,1)} reshape(bf16[16,8,20,1728]{3,2,1,0:T(8,128)(2,1)} %copy.70) | data formatting | bytes 17694720 | tf_op jit(solution)/shard_map/reshape | solution.py:95
  461.0 8.9 %fusion.57 = f32[512,1728]{0,1:T(8,128)S(1)} fusion(bf16[2560,1728]{1,0:T(8,128)(2,1)} %reshape.484, bf16[512,2560]{0,1:T(8,128)(2,1)} %get-tuple-element.184, f32[2560]{0:T(1024)S(1)} %copy-done.7, f32[512]{0:T(512)S(1)} %add_rsqrt_fusion), kind=kOutput, calls=%fused_computation.68 | convolution fusion | flops 4535091200 | bytes 15020032 | tf_op jit(solution)/shard_map/dot_general | solution.py:222
  469.8 7.4 %fusion.51 = bf16[2560,512]{1,0:T(8,128)(2,1)} fusion(bf16[864,2560]{1,0:T(8,128)(2,1)} %param.25, f32[512,1728]{0,1:T(8,128)S(1)} %fusion.57), kind=kOutput, calls=%fused_computation.63 | convolution fusion | flops 2268889088 | bytes 10584064 | tf_op jit(solution)/shard_map/dot_general | solution.py:225
  477.3 61.7 %reduce-scatter.4.cloned.1.call-done = bf16[320,512]{1,0:T(8,128)(2,1)} async-done(((bf16[2560,512]{1,0:T(8,128)(2,1)}), bf16[320,512]{1,0:T(8,128)(2,1)}) %reduce-scatter.4.cloned.1.call-update) | async-done | bytes 327696
  (184 shorter events, 88.6 us)
Async XLA Ops:
  7.4 253.4 %copy-start = (bf16[320,2560]{1,0:T(8,128)(2,1)S(1)}, bf16[320,2560]{1,0:T(8,128)(2,1)}, u32[]{:S(2)}) copy-start(bf16[320,2560]{1,0:T(8,128)(2,1)} %param.24) | copy-start | bytes 4915204
  7.4 5.2 copy-start.3
  7.4 5.3 copy-start.4
  7.4 5.4 copy-start.2
  7.4 164.5 %all-gather.3.cloned.1.call-start = ((), (), s32[]{:S(2)}) async-start(), calls=%async_computation.6 | async-start | bytes 11280384 | tf_op jit(solution)/shard_map/all_gather | solution.py:120
  13.3 10.2 %copy-start.5 = (s32[128]{0:T(128)S(1)}, s32[128]{0:T(128)}, u32[]{:S(2)}) copy-start(s32[128]{0:T(128)} %param.27) | copy-start | bytes 1540
  13.4 11.2 %copy-start.1 = (bf16[2,8,1,80,128]{4,3,2,1,0:T(8,128)(2,1)S(1)}, bf16[2,8,1,80,128]{4,3,2,1,0:T(8,128)(2,1)}, u32[]{:S(2)}) copy-start(bf16[2,8,1,80,128]{4,3,2,1,0:T(8,128)(2,1)} %param.26) | copy-start | bytes 983044
  15.1 53.4 %all-to-all-start = ((bf16[16,20,3840]{2,1,0:T(8,128)(2,1)}), bf16[16,20,3840]{2,1,0:T(8,128)(2,1)}, u32[]{:S(2)}, u32[]{:S(2)}) async-start(bf16[16,20,3840]{2,1,0:T(8,128)(2,1)} %stack.2), calls=%async_computation | async-start | bytes 5898240 | tf_op jit(solution)/shard_map/all_to_all | solution.py:22
  68.5 32.2 %all-to-all-start.2 = ((bf16[2,32,1,80,128]{4,3,0,2,1:T(8,128)(2,1)}), bf16[2,32,1,80,128]{4,3,0,2,1:T(8,128)(2,1)S(1)}, u32[]{:S(2)}, u32[]{:S(2)}) async-start(bf16[2,32,1,80,128]{4,3,0,2,1:T(8,128)(2,1)} %fusion.68), calls=%async_computation.2 | async-start | bytes 2621440 | tf_op jit(solution)/shard_map/all_to_all | solution.py:178
  83.1 25.4 %copy-start.8 = (s32[16]{0:T(128)S(1)}, s32[16]{0:T(128)}, u32[]{:S(2)}) copy-start(s32[16]{0:T(128)} %param.28) | copy-start | bytes 196
  83.1 26.1 %copy-start.9 = (s32[16]{0:T(128)S(1)}, s32[16]{0:T(128)}, u32[]{:S(2)}) copy-start(s32[16]{0:T(128)} %param.29) | copy-start | bytes 196
  100.7 51.4 %all-to-all-start.1 = ((bf16[320,8,480]{2,0,1:T(8,128)(2,1)}), bf16[320,8,480]{2,0,1:T(8,128)(2,1)}, u32[]{:S(2)}, u32[]{:S(2)}) async-start(bf16[320,8,480]{2,0,1:T(8,128)(2,1)} %copy.61), calls=%async_computation.1 | async-start | bytes 5242880 | tf_op jit(solution)/shard_map/all_to_all | solution.py:122
  158.2 5.5 %copy-start.6 = (f32[2560]{0:T(1024)S(1)}, f32[2560]{0:T(1024)}, u32[]{:S(2)}) copy-start(f32[2560]{0:T(1024)} %param.17) | copy-start | bytes 30724
  197.8 226.3 %all-to-all-start.3 = ((bf16[320,8,1728]{2,0,1:T(8,128)(2,1)}), bf16[320,8,1728]{2,0,1:T(8,128)(2,1)}, u32[]{:S(2)}, u32[]{:S(2)}) async-start(bf16[320,8,1728]{2,0,1:T(8,128)(2,1)} %copy.68), calls=%async_computation.3 | async-start | bytes 18350080 | tf_op jit(solution)/shard_map/all_to_all | solution.py:123
  202.8 216.1 %all-reduce.2.cloned.1.call-start = ((), (), s32[]{:S(2)}) async-start(), calls=%async_computation.5 | async-start | bytes 5242880 | tf_op jit(solution)/shard_map/psum | solution.py:219
  263.9 275.1 %reduce-scatter.4.cloned.1.call-start = ((), (), s32[]{:S(2)}) async-start(), calls=%async_computation.7 | async-start | bytes 2949120
  446.6 14.4 %copy-start.7 = (f32[2560]{0:T(1024)S(1)}, f32[2560]{0:T(1024)}, u32[]{:S(2)}) copy-start(f32[2560]{0:T(1024)} %param.18) | copy-start | bytes 30724
Sparse Core Ops, SparseCore 0:
  12.6 138.0 all-gather.2
Sparse Core Ops, SparseCore 1:
  264.0 154.9 all-reduce.1
  477.4 61.6 reduce-scatter.3
